TPU v7x, 256 devices: a whole 4x4x8 slice. The times are simulated.
256 devices in a mesh: space: 16 (over x, z_hi), tm: 16 (over y, z_lo, core).
Axes of the slice: x: 4, y: 4, z: 8 (z_hi: 4, z_lo: 2; z = z_hi * 2 + z_lo), core: 2. Of those that a mesh axis runs over, the one named last changes fastest.
Arguments:
- latent: float32 [24, 1024, 2048], P(None, 'space', 'tm'), may hold values from -1.8 to 1.8
- events: int32 [24, 1024, 2048], P(None, 'space', 'tm'), may hold values from 0 to 7
- log_base: float32 [24, 1024, 2048], P(None, 'space', 'tm'), may hold values from -1.5 to 0.5
- innovation: float32 [24, 1024, 2048], P(None, 'space', 'tm'), may hold values from -6 to 6
- kappa_sq: float32 [24, 1024], replicated, may hold values from 0.3 to 3
- chol_factor: float32 [2048, 2048], P(None, 'tm'), as said below
- step_size: float32 [1], replicated, may hold values from 0.02 to 0.08
Outputs:
- gradient: float32 [24, 1024, 2048], P(None, 'space', 'tm')
- proposal: float32 [24, 1024, 2048], P(None, 'space', 'tm')
Inputs may be any that keep to these rules, and one draw needn't show every extreme that they name: chol_factor is lower triangular with a positive diagonal.
All inputs are finite; a program needn't handle non-finite values.
Results may differ from a plain program's by a relative error of at most 0.000067.
Values sent between devices are 32-bit elements; how exact they have to be, the bound alone decides.
A program may use at most 64 MiB of HBM per device.

v0:
```python
import jax
import jax.numpy as jnp
from jax import lax
from jax.sharding import PartitionSpec as P


def padded(block, sides, width):
    for axis, dim in sides:
        count = lax.axis_size(axis)
        forward = [(i, i + 1) for i in range(count - 1)]
        backward = [(target, source) for source, target in forward]
        low = lax.ppermute(
            lax.slice_in_dim(block, block.shape[dim] - width, None, axis=dim), axis, forward
        )
        high = lax.ppermute(lax.slice_in_dim(block, 0, width, axis=dim), axis, backward)
        block = jnp.concatenate([low, block, high], axis=dim)
    return block


def operate(extended, kappa_cols):
    centre = extended[:, 1:-1]
    row_padded = jnp.pad(centre, ((1, 1), (0, 0), (0, 0)))
    beside = row_padded[2:] + row_padded[:-2]
    beside = beside + extended[:, 2:] + extended[:, :-2]
    return (kappa_cols[:, :, None] + 4.0) * centre - beside


def face_halo(field):
    return padded(field, (("space", 1),), 1)


def local(latent, events, log_base, innovation, kappa_sq, chol_factor, step_size):
    row_count, col_count, time_count = latent.shape
    col_index = lax.axis_index("space")
    padded_kappa = jnp.pad(kappa_sq, ((0, 0), (2, 2)))
    first_col = col_index * col_count + 2 - 0
    kappa_here = lax.dynamic_slice(
        padded_kappa, (jnp.int32(0), first_col), (row_count, col_count + 2 * 0)
    )
    first_pass = operate(face_halo(latent), kappa_here)
    spatial = operate(face_halo(first_pass), kappa_here)
    cell_count = row_count * col_count
    flattened = spatial.reshape(cell_count, time_count)
    factor_rows = chol_factor
    projected = jnp.dot(
        lax.all_gather(flattened, "tm", axis=1, tiled=True),
        factor_rows,
        precision=lax.Precision.HIGHEST,
        preferred_element_type=jnp.float32,
    )
    factor_rows = chol_factor
    by_hour = lax.psum_scatter(
        lax.dot_general(
            factor_rows,
            projected,
            (((1,), (1,)), ((), ())),
            precision=lax.Precision.HIGHEST,
            preferred_element_type=jnp.float32,
        ),
        "tm",
        scatter_dimension=0,
        tiled=True,
    )
    prior_term = by_hour.T.reshape(row_count, col_count, time_count)
    gradient = events.astype(jnp.float32) - jnp.exp(log_base + latent) - prior_term
    proposal = latent + step_size[0] * gradient + jnp.sqrt(2.0 * step_size[0]) * innovation
    return (gradient, proposal)


def solution(mesh):
    in_specs = (
        P(None, "space", "tm"),
        P(None, "space", "tm"),
        P(None, "space", "tm"),
        P(None, "space", "tm"),
        P(),
        P(None, "tm"),
        P(),
    )
    out_specs = (P(None, "space", "tm"), P(None, "space", "tm"))
    return jax.shard_map(local, mesh=mesh, in_specs=in_specs, out_specs=out_specs, check_vma=False)
```

profile of v0, /device:TPU:2, one launch (start us, length us, event | category | flops | bytes accessed | tf_op | source)
XLA Modules:
  0.0 296.3 jit_solution(11682274919811678598)
XLA Ops:
  7.2 0.0 copy-start
  7.2 0.0 all-gather.2.cloned.1.call-start
  7.2 1.0 fusion.10
  8.3 8.2 %collective-permute-start = (f32[24,1,128]{2,1,0:T(1,128)S(1)}, f32[24,1,128]{2,1,0:T(1,128)S(1)}, u32[]{:S(2)}, u32[]{:S(2)}) collective-permute-start(f32[24,1,128]{2,1,0:T(1,128)S(1)} %get-tuple-element.6), channel_id=1, source_target_pairs={{16,0},{32,16},{48,32},{64,48},{80,64},{96,80},{112,96},{128,112},... | collective-permute-start | bytes 36872 | tf_op jit(solution)/shard_map/ppermute | solution.py:15
  16.5 1.9 collective-permute-start.1
  18.4 0.9 fusion.8
  19.2 0.0 collective-permute-done
  19.2 5.8 %collective-permute-done.1 = f32[24,1,128]{2,1,0:T(1,128)S(1)} collective-permute-done((f32[24,1,128]{2,1,0:T(1,128)S(1)}, f32[24,1,128]{2,1,0:T(1,128)S(1)}, u32[]{:S(2)}, u32[]{:S(2)}) %collective-permute-start.1) | collective-permute-done | bytes 12320 | tf_op jit(solution)/shard_map/ppermute | solution.py:12
  25.1 2.9 fusion.3
  28.0 1.9 collective-permute-start.2
  29.9 4.8 %collective-permute-start.3 = (f32[24,1,128]{2,1,0:T(1,128)S(1)}, f32[24,1,128]{2,1,0:T(1,128)S(1)}, u32[]{:S(2)}, u32[]{:S(2)}) collective-permute-start(f32[24,1,128]{2,1,0:T(1,128)S(1)} %get-tuple-element.5), channel_id=1, source_target_pairs={{0,16},{16,32},{32,48},{48,64},{64,80},{80,96},{96,112},{112,128},... | collective-permute-start | bytes 36872 | tf_op jit(solution)/shard_map/ppermute | solution.py:12
  34.7 0.0 collective-permute-done.2
  34.7 3.8 %collective-permute-done.3 = f32[24,1,128]{2,1,0:T(1,128)S(1)} collective-permute-done((f32[24,1,128]{2,1,0:T(1,128)S(1)}, f32[24,1,128]{2,1,0:T(1,128)S(1)}, u32[]{:S(2)}, u32[]{:S(2)}) %collective-permute-start.3) | collective-permute-done | bytes 12320 | tf_op jit(solution)/shard_map/ppermute | solution.py:12
  38.5 1.2 fusion.7
  39.7 0.0 all-gather.2.cloned.1.call-update
  39.7 0.0 reduce-scatter.2.cloned.1.call-start
  39.8 79.2 %all-gather.2.cloned.1.call-done = f32[1536,2048]{1,0:T(8,128)} async-done(((f32[1536,128]{1,0:T(8,128)}), f32[1536,2048]{1,0:T(8,128)}) %all-gather.2.cloned.1.call-update) | async-done | bytes 12582928 | tf_op jit(solution)/shard_map/all_gather | solution.py:46
  119.0 0.0 copy-done
  119.0 12.5 %fusion.11 = f32[1536,128]{1,0:T(8,128)S(1)} fusion(f32[1536,2048]{1,0:T(8,128)} %all-gather.2.cloned.1.call-done, f32[2048,128]{1,0:T(8,128)S(1)} %copy-done), kind=kOutput, calls=%fused_computation.23 | convolution fusion | flops 4831838208 | bytes 14417920 | tf_op jit(solution)/shard_map/dot_general | solution.py:45
  131.5 0.0 copy-start.1
  131.5 0.0 copy-start.2
  131.5 0.0 copy-start.3
  131.5 12.3 %convolution_bitcast_fusion = f32[2048,1536]{0,1:T(8,128)} fusion(f32[1536,128]{1,0:T(8,128)S(1)} %fusion.11, f32[2048,128]{1,0:T(8,128)S(1)} %copy-done), kind=kOutput, calls=%fused_computation | convolution fusion | flops 4831838208 | bytes 14417920 | tf_op jit(solution)/shard_map/dot_general | solution.py:53
  143.8 0.0 reduce-scatter.2.cloned.1.call-update
  144.5 142.1 %reduce-scatter.2.cloned.1.call-done = f32[128,1536]{0,1:T(8,128)} async-done(((f32[2048,1536]{0,1:T(8,128)}), f32[128,1536]{0,1:T(8,128)}) %reduce-scatter.2.cloned.1.call-update) | async-done | bytes 786448 | tf_op jit(solution)/shard_map/reduce_scatter | solution.py:52
  286.6 0.0 copy-done.1
  286.6 0.0 copy-done.2
  286.6 0.0 copy-done.3
  286.6 2.9 multiply_add_fusion
  (1 shorter events, 0.0 us)
Async XLA Ops:
  7.2 111.8 %copy-start = (f32[2048,128]{1,0:T(8,128)S(1)}, f32[2048,128]{1,0:T(8,128)}, u32[]{:S(2)}) copy-start(f32[2048,128]{1,0:T(8,128)} %param.12) | copy-start | bytes 3145732
  7.2 111.8 %all-gather.2.cloned.1.call-start = ((), (), s32[]{:S(2)}) async-start(), calls=%async_computation.1 | async-start | bytes 13369344 | tf_op jit(solution)/shard_map/all_gather | solution.py:46
  8.3 11.0 %collective-permute-start = (f32[24,1,128]{2,1,0:T(1,128)S(1)}, f32[24,1,128]{2,1,0:T(1,128)S(1)}, u32[]{:S(2)}, u32[]{:S(2)}) collective-permute-start(f32[24,1,128]{2,1,0:T(1,128)S(1)} %get-tuple-element.6), channel_id=1, source_target_pairs={{16,0},{32,16},{48,32},{64,48},{80,64},{96,80},{112,96},{128,112},... | collective-permute-start | bytes 36872 | tf_op jit(solution)/shard_map/ppermute | solution.py:15
  16.5 8.6 %collective-permute-start.1 = (f32[24,1,128]{2,1,0:T(1,128)S(1)}, f32[24,1,128]{2,1,0:T(1,128)S(1)}, u32[]{:S(2)}, u32[]{:S(2)}) collective-permute-start(f32[24,1,128]{2,1,0:T(1,128)S(1)} %get-tuple-element.7), channel_id=1, source_target_pairs={{0,16},{16,32},{32,48},{48,64},{64,80},{80,96},{96,112},{112,128},... | collective-permute-start | bytes 36872 | tf_op jit(solution)/shard_map/ppermute | solution.py:12
  28.0 6.8 %collective-permute-start.2 = (f32[24,1,128]{2,1,0:T(1,128)S(1)}, f32[24,1,128]{2,1,0:T(1,128)S(1)}, u32[]{:S(2)}, u32[]{:S(2)}) collective-permute-start(f32[24,1,128]{2,1,0:T(1,128)S(1)} %get-tuple-element.4), channel_id=1, source_target_pairs={{16,0},{32,16},{48,32},{64,48},{80,64},{96,80},{112,96},{128,112},... | collective-permute-start | bytes 36872 | tf_op jit(solution)/shard_map/ppermute | solution.py:15
  29.9 8.6 %collective-permute-start.3 = (f32[24,1,128]{2,1,0:T(1,128)S(1)}, f32[24,1,128]{2,1,0:T(1,128)S(1)}, u32[]{:S(2)}, u32[]{:S(2)}) collective-permute-start(f32[24,1,128]{2,1,0:T(1,128)S(1)} %get-tuple-element.5), channel_id=1, source_target_pairs={{0,16},{16,32},{32,48},{48,64},{64,80},{80,96},{96,112},{112,128},... | collective-permute-start | bytes 36872 | tf_op jit(solution)/shard_map/ppermute | solution.py:12
  39.7 246.9 %reduce-scatter.2.cloned.1.call-start = ((), (), s32[]{:S(2)}) async-start(), calls=%async_computation.2 | async-start | bytes 13369344 | tf_op jit(solution)/shard_map/reduce_scatter | solution.py:52
  131.5 155.1 %copy-start.1 = (f32[24,64,128]{2,1,0:T(8,128)S(1)}, f32[24,64,128]{2,1,0:T(8,128)}, u32[]{:S(2)}) copy-start(f32[24,64,128]{2,1,0:T(8,128)} %param.7) | copy-start | bytes 2359300
  131.5 155.1 %copy-start.2 = (f32[24,64,128]{2,1,0:T(8,128)S(1)}, f32[24,64,128]{2,1,0:T(8,128)}, u32[]{:S(2)}) copy-start(f32[24,64,128]{2,1,0:T(8,128)} %param.10) | copy-start | bytes 2359300
  131.5 155.1 %copy-start.3 = (f32[24,64,128]{2,1,0:T(8,128)S(1)}, f32[24,64,128]{2,1,0:T(8,128)}, u32[]{:S(2)}) copy-start(f32[24,64,128]{2,1,0:T(8,128)} %param.9) | copy-start | bytes 2359300
Sparse Core Ops, SparseCore 0:
  39.8 79.1 all-gather.1
  143.9 142.5 reduce-scatter.1
where the time goes:
time: 297 us; the launch traced here: 296 us
  waiting for transfers between devices  231 us (78%)
  matrix products  24.8 us (8%)
  starting transfers between devices  16.9 us (6%)
  between operations  14.8 us (5%)
  other arithmetic  7.85 us (3%)
    reduce_scatter x1, waiting for transfers between devices, local(): lax.psum_scatter(lax.dot_general(factor_rows, projected, (((1,), (1,)), (...  142 us
    all_gather x1, waiting for transfers between devices, local(): lax.all_gather(flattened, 'tm', axis=1, tiled=True)  79.2 us
    dot_general x1, matrix products, local(): jnp.dot(lax.all_gather(flattened, 'tm', axis=1, tiled=True), factor_rows,...  12.5 us
    dot_general x1, matrix products, local(): lax.dot_general(factor_rows, projected, (((1,), (1,)), ((), ())), precisi...  12.3 us
    ppermute x2, starting transfers between devices, padded(): lax.ppermute(lax.slice_in_dim(block, 0, width, axis=dim), axis, backward)  10.1 us
    ppermute x2, waiting for transfers between devices, padded(): lax.ppermute(lax.slice_in_dim(block, block.shape[dim] - width, None, axis...  9.56 us
    ppermute x2, starting transfers between devices, padded(): lax.ppermute(lax.slice_in_dim(block, block.shape[dim] - width, None, axis...  6.74 us
  transfers between devices with their start and end apart: 6, of which 4 were waited for; matrix products, arithmetic and copies ran while one was open for 0% of the time, Pallas kernels for 0%

commit v1 on v0

--- a/solution.py
+++ b/solution.py
@@ -2,6 +2,7 @@
 import jax.numpy as jnp
 from jax import lax
 from jax.sharding import PartitionSpec as P
+from jax.lax import all_to_all, axis_size
 
 
 def padded(block, sides, width):
@@ -43,7 +44,15 @@
     flattened = spatial.reshape(cell_count, time_count)
     factor_rows = chol_factor
     projected = jnp.dot(
-        lax.all_gather(flattened, "tm", axis=1, tiled=True),
+        jnp.concatenate(
+            all_to_all(
+                jnp.stack([flattened for _ in range(axis_size("tm"))]),
+                axis_name="tm",
+                split_axis=0,
+                concat_axis=0,
+            ),
+            axis=1,
+        ),
         factor_rows,
         precision=lax.Precision.HIGHEST,
         preferred_element_type=jnp.float32,

time: 297 us -> 366 us (1.23)
  blocking collectives: 0 us -> 145 us
  waiting for transfers between devices: 231 us -> 147 us
  matrix products: 24.8 us -> 33.1 us
    all_to_all x0 -> x1, blocking collectives: none -> 145 us  [local(): all_to_all(jnp.stack([flattened for _ in range(axis_size('tm'))]), axis_n...]
    all_gather x1 -> x0, waiting for transfers between devices: 79.2 us -> none  [local(): lax.all_gather(flattened, 'tm', axis=1, tiled=True)]
    dot_general x1, matrix products: 12.5 us -> 20.8 us  [local(): jnp.dot(jnp.concatenate(all_to_all(jnp.stack([flattened for _ in range(ax...]
    reduce_scatter x1, waiting for transfers between devices: 142 us -> 137 us  [local(): lax.psum_scatter(lax.dot_general(factor_rows, projected, (((1,), (1,)), (...]
  transfers between devices with their start and end apart: 6 -> 5, of which waited for: 4 -> 3; matrix products, arithmetic and copies ran while one was open for 0% -> 0% of each run, Pallas kernels for 0% -> 0%
where the time goes in v1:
time: 366 us
  waiting for transfers between devices  147 us (40%)
  blocking collectives  145 us (40%)
  matrix products  33.1 us (9%)
  starting transfers between devices  16.9 us (5%)
  between operations  14.8 us (4%)
  other arithmetic  6.8 us (2%)
    all_to_all x1, blocking collectives, local(): all_to_all(jnp.stack([flattened for _ in range(axis_size('tm'))]), axis_n...  145 us
    reduce_scatter x1, waiting for transfers between devices, local(): lax.psum_scatter(lax.dot_general(factor_rows, projected, (((1,), (1,)), (...  137 us
    dot_general x1, matrix products, local(): jnp.dot(jnp.concatenate(all_to_all(jnp.stack([flattened for _ in range(ax...  20.8 us
    dot_general x1, matrix products, local(): lax.dot_general(factor_rows, projected, (((1,), (1,)), ((), ())), precisi...  12.3 us
    ppermute x2, starting transfers between devices, padded(): lax.ppermute(lax.slice_in_dim(block, 0, width, axis=dim), axis, backward)  10.1 us
    ppermute x2, waiting for transfers between devices, padded(): lax.ppermute(lax.slice_in_dim(block, block.shape[dim] - width, None, axis...  9.56 us
  transfers between devices with their start and end apart: 5, of which 3 were waited for; matrix products, arithmetic and copies ran while one was open for 0% of the time, Pallas kernels for 0%

profile of v1, /device:TPU:2, one launch (start us, length us, event | category | flops | bytes accessed | tf_op | source)
XLA Modules:
  0.0 366.1 jit_solution(8558825349638186980)
XLA Ops:
  7.2 0.0 copy-start
  7.2 0.0 reduce-scatter.2.cloned.1.call-start
  7.2 1.0 fusion.10
  8.3 8.2 %collective-permute-start = (f32[24,1,128]{2,1,0:T(1,128)S(1)}, f32[24,1,128]{2,1,0:T(1,128)S(1)}, u32[]{:S(2)}, u32[]{:S(2)}) collective-permute-start(f32[24,1,128]{2,1,0:T(1,128)S(1)} %get-tuple-element.6), channel_id=1, source_target_pairs={{16,0},{32,16},{48,32},{64,48},{80,64},{96,80},{112,96},{128,112},... | collective-permute-start | bytes 36872 | tf_op jit(solution)/shard_map/ppermute | solution.py:16
  16.5 1.9 collective-permute-start.1
  18.4 0.9 fusion.8
  19.2 0.0 collective-permute-done
  19.2 5.8 %collective-permute-done.1 = f32[24,1,128]{2,1,0:T(1,128)S(1)} collective-permute-done((f32[24,1,128]{2,1,0:T(1,128)S(1)}, f32[24,1,128]{2,1,0:T(1,128)S(1)}, u32[]{:S(2)}, u32[]{:S(2)}) %collective-permute-start.1) | collective-permute-done | bytes 12320 | tf_op jit(solution)/shard_map/ppermute | solution.py:13
  25.1 2.7 fusion.3
  27.8 1.9 collective-permute-start.2
  29.7 4.8 %collective-permute-start.3 = (f32[24,1,128]{2,1,0:T(1,128)S(1)}, f32[24,1,128]{2,1,0:T(1,128)S(1)}, u32[]{:S(2)}, u32[]{:S(2)}) collective-permute-start(f32[24,1,128]{2,1,0:T(1,128)S(1)} %get-tuple-element.5), channel_id=1, source_target_pairs={{0,16},{16,32},{32,48},{48,64},{64,80},{80,96},{96,112},{112,128},... | collective-permute-start | bytes 36872 | tf_op jit(solution)/shard_map/ppermute | solution.py:13
  34.5 0.0 collective-permute-done.2
  34.5 3.8 %collective-permute-done.3 = f32[24,1,128]{2,1,0:T(1,128)S(1)} collective-permute-done((f32[24,1,128]{2,1,0:T(1,128)S(1)}, f32[24,1,128]{2,1,0:T(1,128)S(1)}, u32[]{:S(2)}, u32[]{:S(2)}) %collective-permute-start.3) | collective-permute-done | bytes 12320 | tf_op jit(solution)/shard_map/ppermute | solution.py:13
  38.3 0.3 fusion.7
  38.6 0.3 copy.9
  38.9 1.6 stack.3
  40.5 144.9 %all_to_all.5 = f32[16,1536,128]{1,2,0:T(8,128)S(1)} all-to-all(f32[16,1536,128]{1,2,0:T(8,128)S(1)} %stack.3), channel_id=1, replica_groups=mesh['space'=16,'tm'=16] {'tm'}, dimensions={0} | all-to-all | bytes 25165824 | tf_op jit(solution)/shard_map/all_to_all | solution.py:48
  185.4 0.0 copy-done
  185.4 20.8 %fusion.11 = f32[1536,128]{1,0:T(8,128)S(1)} fusion(f32[1536,2048]{0,1:T(8,128)S(1)} %bitcast.16, f32[2048,128]{1,0:T(8,128)S(1)} %copy-done), kind=kOutput, calls=%fused_computation.23 | convolution fusion | flops 4831838208 | bytes 14417920 | tf_op jit(solution)/shard_map/dot_general | solution.py:46
  206.2 0.0 copy-start.1
  206.2 0.0 copy-start.2
  206.2 0.0 copy-start.3
  206.2 12.3 %convolution_bitcast_fusion = f32[2048,1536]{0,1:T(8,128)} fusion(f32[1536,128]{1,0:T(8,128)S(1)} %fusion.11, f32[2048,128]{1,0:T(8,128)S(1)} %copy-done), kind=kOutput, calls=%fused_computation | convolution fusion | flops 4831838208 | bytes 14417920 | tf_op jit(solution)/shard_map/dot_general | solution.py:62
  218.5 0.0 reduce-scatter.2.cloned.1.call-update
  219.2 137.1 %reduce-scatter.2.cloned.1.call-done = f32[128,1536]{0,1:T(8,128)} async-done(((f32[2048,1536]{0,1:T(8,128)}), f32[128,1536]{0,1:T(8,128)}) %reduce-scatter.2.cloned.1.call-update) | async-done | bytes 786448 | tf_op jit(solution)/shard_map/reduce_scatter | solution.py:61
  356.3 0.0 copy-done.1
  356.3 0.0 copy-done.2
  356.3 0.0 copy-done.3
  356.3 2.9 multiply_add_fusion
  (1 shorter events, 0.0 us)
Async XLA Ops:
  7.2 178.2 %copy-start = (f32[2048,128]{1,0:T(8,128)S(1)}, f32[2048,128]{1,0:T(8,128)}, u32[]{:S(2)}) copy-start(f32[2048,128]{1,0:T(8,128)} %param.12) | copy-start | bytes 3145732
  7.2 349.1 %reduce-scatter.2.cloned.1.call-start = ((), (), s32[]{:S(2)}) async-start(), calls=%async_computation.2 | async-start | bytes 13369344 | tf_op jit(solution)/shard_map/reduce_scatter | solution.py:61
  8.3 11.0 %collective-permute-start = (f32[24,1,128]{2,1,0:T(1,128)S(1)}, f32[24,1,128]{2,1,0:T(1,128)S(1)}, u32[]{:S(2)}, u32[]{:S(2)}) collective-permute-start(f32[24,1,128]{2,1,0:T(1,128)S(1)} %get-tuple-element.6), channel_id=1, source_target_pairs={{16,0},{32,16},{48,32},{64,48},{80,64},{96,80},{112,96},{128,112},... | collective-permute-start | bytes 36872 | tf_op jit(solution)/shard_map/ppermute | solution.py:16
  16.5 8.6 %collective-permute-start.1 = (f32[24,1,128]{2,1,0:T(1,128)S(1)}, f32[24,1,128]{2,1,0:T(1,128)S(1)}, u32[]{:S(2)}, u32[]{:S(2)}) collective-permute-start(f32[24,1,128]{2,1,0:T(1,128)S(1)} %get-tuple-element.7), channel_id=1, source_target_pairs={{0,16},{16,32},{32,48},{48,64},{64,80},{80,96},{96,112},{112,128},... | collective-permute-start | bytes 36872 | tf_op jit(solution)/shard_map/ppermute | solution.py:13
  27.8 6.8 %collective-permute-start.2 = (f32[24,1,128]{2,1,0:T(1,128)S(1)}, f32[24,1,128]{2,1,0:T(1,128)S(1)}, u32[]{:S(2)}, u32[]{:S(2)}) collective-permute-start(f32[24,1,128]{2,1,0:T(1,128)S(1)} %get-tuple-element.4), channel_id=1, source_target_pairs={{16,0},{32,16},{48,32},{64,48},{80,64},{96,80},{112,96},{128,112},... | collective-permute-start | bytes 36872 | tf_op jit(solution)/shard_map/ppermute | solution.py:16
  29.7 8.6 %collective-permute-start.3 = (f32[24,1,128]{2,1,0:T(1,128)S(1)}, f32[24,1,128]{2,1,0:T(1,128)S(1)}, u32[]{:S(2)}, u32[]{:S(2)}) collective-permute-start(f32[24,1,128]{2,1,0:T(1,128)S(1)} %get-tuple-element.5), channel_id=1, source_target_pairs={{0,16},{16,32},{32,48},{48,64},{64,80},{80,96},{96,112},{112,128},... | collective-permute-start | bytes 36872 | tf_op jit(solution)/shard_map/ppermute | solution.py:13
  206.2 150.1 %copy-start.1 = (f32[24,64,128]{2,1,0:T(8,128)S(1)}, f32[24,64,128]{2,1,0:T(8,128)}, u32[]{:S(2)}) copy-start(f32[24,64,128]{2,1,0:T(8,128)} %param.7) | copy-start | bytes 2359300
  206.2 150.1 %copy-start.2 = (f32[24,64,128]{2,1,0:T(8,128)S(1)}, f32[24,64,128]{2,1,0:T(8,128)}, u32[]{:S(2)}) copy-start(f32[24,64,128]{2,1,0:T(8,128)} %param.10) | copy-start | bytes 2359300
  206.2 150.1 %copy-start.3 = (f32[24,64,128]{2,1,0:T(8,128)S(1)}, f32[24,64,128]{2,1,0:T(8,128)}, u32[]{:S(2)}) copy-start(f32[24,64,128]{2,1,0:T(8,128)} %param.9) | copy-start | bytes 2359300
Sparse Core Ops, SparseCore 0:
  218.7 137.6 reduce-scatter.1
